TPU v7x, 512 devices: a whole 4x4x16 slice. The times are simulated.
512 devices in a mesh: space: 32 (over z, x_lo), field: 16 (over x_hi, y, core).
Axes of the slice: x: 4 (x_hi: 2, x_lo: 2; x = x_hi * 2 + x_lo), y: 4, z: 16, core: 2. Of those that a mesh axis runs over, the one named last changes fastest.
Arguments:
- composition_vector: float32 [16, 32, 128, 16, 128], P('field', None, 'space'), may hold values from -6 to 6
- filtered_motion: float32 [3, 128, 16, 128], P(None, 'space', 'field'), may hold values from -1.8 to 1.8
- spreading_strength: float32 [128, 16, 128], P('space', 'field'), may hold values from 0.02 to 0.12
- blend_relax_multiplier: float32 [128, 16, 128], P('space', 'field'), may hold values from 0.2 to 0.9
- thermal_level: float32 [128, 16, 128], P('space', 'field'), may hold values from 0.5 to 2
- brownian_jumps: float32 [2, 16, 3], P(None, 'field'), may hold values from -2.5 to 2.5
- left_bilinear_weights: bfloat16 [206, 32], replicated, may hold values from -1 to 1
- right_bilinear_weights: bfloat16 [206, 32], replicated, may hold values from -1 to 1
- species_yield_weights: bfloat16 [32, 206], replicated, may hold values from -0.4375 to 0.4375
- arrhenius_prefactor: float32 [206], replicated, may hold values from 0.3 to 3
- ignition_energy_ratio: float32 [206], replicated, may hold values from 0.2 to 2
Outputs:
- result: float32 [16, 32, 128, 16, 128], P('field', None, 'space')
All inputs are finite; a program needn't handle non-finite values.
Results may differ from a plain program's by a relative error of at most 0.00068.
Values sent between devices are 32-bit elements; how exact they have to be, the bound alone decides.
No kernel may reach another device: no remote copies, remote signals or barrier semaphores. Data moves between devices by JAX's collectives and lax.ppermute only.
A program may use at most 64 MiB of HBM per device.

v0:
```python
import jax
import jax.numpy as jnp
from jax import lax
from jax.sharding import PartitionSpec as P

STEPS = 2
SUB = 5
chem_step = 0.2


def turned_gather(arrays, axis, dims):
    turned = [jnp.moveaxis(a, dim, 0) for a, dim in zip(arrays, dims)]
    widths = [t[0].size for t in turned]
    both = jnp.concatenate([t.reshape(-1, w) for t, w in zip(turned, widths)], axis=1)
    result = lax.all_gather(both, axis, axis=0, tiled=True)
    tiles = jnp.split(result, [sum(widths[:k]) for k in range(1, len(widths))], axis=1)
    return tuple(
        (
            jnp.moveaxis(b.reshape(-1, *t.shape[1:]), 0, dim)
            for b, t, dim in zip(tiles, turned, dims)
        )
    )


def split_up(value, dim, count):
    dims = value.shape
    tiles = value.reshape(*dims[:dim], count, dims[dim] // count, *dims[dim + 1 :])
    return jnp.moveaxis(tiles, dim, 0)


def sent_and_summed(value, axis, dim):
    tiles = split_up(value, dim, lax.axis_size(axis))
    arrived = lax.all_to_all(tiles, axis, split_axis=0, concat_axis=0, tiled=True)
    return arrived.sum(axis=0)


def laid_out(tiles, dim):
    dims = list(tiles.shape[1:])
    dims[dim] *= tiles.shape[0]
    return jnp.moveaxis(tiles, 0, dim).reshape(dims)


def from_everyone(value, axis):
    count = lax.axis_size(axis)
    return lax.all_to_all(
        jnp.broadcast_to(value[None], (count, *value.shape)), axis, 0, 0, tiled=True
    )


def collect(value, axis, dim):
    return laid_out(from_everyone(value, axis), dim)


def extended(value, sides, width):
    for axis, dim in sides:
        count, length = (lax.axis_size(axis), value.shape[dim])
        up = [(i, (i + 1) % count) for i in range(count)]
        down = [(j, i) for i, j in up]
        last = lax.slice_in_dim(value, length - width, length, axis=dim)
        leading = lax.slice_in_dim(value, 0, width, axis=dim)
        before = lax.ppermute(last, axis, up)
        after = lax.ppermute(leading, axis, down)
        value = jnp.concatenate([before, value, after], axis=dim)
    return value


def transport(padded, current, mean, filtered_motion, spreading_strength, mixing, wiener):
    x_plus = padded[:, 2:]
    x_minus = padded[:, :-2]
    y_plus = jnp.roll(current, -1, 2)
    y_minus = jnp.roll(current, 1, 2)
    z_plus = jnp.roll(current, -1, 3)
    z_minus = jnp.roll(current, 1, 3)
    grad_x = 0.5 * (x_plus - x_minus)
    grad_y = 0.5 * (y_plus - y_minus)
    grad_z = 0.5 * (z_plus - z_minus)
    laplace = x_plus + x_minus + y_plus + y_minus + z_plus + z_minus - 6.0 * current
    advect = filtered_motion[0] * grad_x + filtered_motion[1] * grad_y + filtered_motion[2] * grad_z
    noise = jnp.sqrt(2.0 * spreading_strength) * (
        wiener[0] * grad_x + wiener[1] * grad_y + wiener[2] * grad_z
    )
    return current - advect + spreading_strength * laplace + noise - mixing * (current - mean)


def react(block, arrhenius, left_bilinear_weights, right_bilinear_weights, species_yield_weights):
    for substep in range(SUB):
        lowered = block.astype(jnp.bfloat16)
        forward = jnp.dot(left_bilinear_weights, lowered, preferred_element_type=jnp.float32)
        backward = jnp.dot(right_bilinear_weights, lowered, preferred_element_type=jnp.float32)
        saturation = 1.0 + forward * forward + backward * backward
        rates = (arrhenius * forward * backward / saturation).astype(jnp.bfloat16)
        block = block + chem_step * jnp.dot(
            species_yield_weights, rates, preferred_element_type=jnp.float32
        )
    return block


def kinetic_yield_term(
    carried_ensemble,
    thermal_level,
    arrhenius_prefactor,
    ignition_energy_ratio,
    left_bilinear_weights,
    right_bilinear_weights,
    species_yield_weights,
):
    species_count, planes, vertical_extent, streamwise_extent = carried_ensemble.shape

    def one_plane(plane_index, current):
        starting_ensemble = jnp.asarray(plane_index).astype(jnp.int32)
        block = lax.dynamic_slice_in_dim(current, starting_ensemble, 1, 1).reshape(
            species_count, vertical_extent * streamwise_extent
        )
        enthalpy_output = lax.dynamic_slice_in_dim(thermal_level, starting_ensemble, 1, 0).reshape(
            1, vertical_extent * streamwise_extent
        )
        arrhenius = arrhenius_prefactor[:, None] * jnp.exp(
            -ignition_energy_ratio[:, None] / enthalpy_output
        )
        reacted = react(
            block, arrhenius, left_bilinear_weights, right_bilinear_weights, species_yield_weights
        )
        reacted = reacted.reshape(species_count, 1, vertical_extent, streamwise_extent)
        return lax.dynamic_update_slice_in_dim(current, reacted, starting_ensemble, 1)

    return lax.fori_loop(0, planes, one_plane, carried_ensemble)


def body(
    composition_vector,
    filtered_motion,
    spreading_strength,
    blend_relax_multiplier,
    thermal_level,
    brownian_jumps,
    left_bilinear_weights,
    right_bilinear_weights,
    species_yield_weights,
    arrhenius_prefactor,
    ignition_energy_ratio,
):
    fields = lax.axis_size("field")
    motion_lookup, spreading_gradient_sum, subgrid_blend_sum, thermal_lookup = turned_gather(
        (filtered_motion, spreading_strength, blend_relax_multiplier, thermal_level),
        "field",
        (2, 1, 1, 1),
    )
    current = composition_vector[0]
    for step in range(STEPS):
        share = sent_and_summed(current, "field", 2) / fields
        mean = collect(share, "field", 2)
        padded = extended(current, (("space", 1),), 1)
        carried_ensemble = transport(
            padded,
            current,
            mean,
            motion_lookup,
            spreading_gradient_sum,
            subgrid_blend_sum,
            brownian_jumps[step, 0],
        )
        current = kinetic_yield_term(
            carried_ensemble,
            thermal_lookup,
            arrhenius_prefactor,
            ignition_energy_ratio,
            left_bilinear_weights,
            right_bilinear_weights,
            species_yield_weights,
        )
    return current[None]


def solution(mesh):
    return jax.shard_map(
        body,
        mesh=mesh,
        in_specs=(
            P("field", None, "space", None, None),
            P(None, "space", "field", None),
            P("space", "field", None),
            P("space", "field", None),
            P("space", "field", None),
            P(None, "field", None),
            P(),
            P(),
            P(),
            P(),
            P(),
        ),
        out_specs=P("field", None, "space", None, None),
        check_vma=False,
    )
```

profile of v0, /device:TPU:6, one launch (start us, length us, event | category | flops | bytes accessed | tf_op | source)
XLA Modules:
  0.0 205.6 jit_solution(5558131106530953683)
XLA Ops:
  0.0 2.7 %copy.133 = f32[1,32,4,16,128]{4,2,1,3,0:T(4,128)} copy(f32[1,32,4,16,128]{4,3,2,1,0:T(8,128)} %param.15) | data formatting | bytes 2097152 | tf_op args[0]
  2.7 7.5 %all-to-all-start = ((f32[16,32,4,1,128]{4,2,1,3,0:T(4,128)}), f32[16,32,4,1,128]{4,2,1,3,0:T(4,128)S(1)}, u32[]{:S(2)}, u32[]{:S(2)}) async-start(f32[16,32,4,1,128]{4,2,1,3,0:T(4,128)} %bitcast.249), calls=%async_computation | async-start | bytes 2097152 | tf_op jit(solution)/shard_map/all_to_all | solution.py:33
  11.7 4.6 %collective-permute-start = (f32[32,1,16,128]{3,0,1,2:T(8,128)}, f32[32,1,16,128]{3,0,1,2:T(8,128)}, u32[]{:S(2)}, u32[]{:S(2)}) collective-permute-start(f32[32,1,16,128]{3,0,1,2:T(8,128)} %get-tuple-element.496), channel_id=1, source_target_pairs={{16,0},{32,16},{48,32},{64,48},{80,64},{96,80},{112,96},{128,112},... | collective-permute-start | bytes 786440 | tf_op jit(solution)/shard_map/ppermute | solution.py:62
  16.3 2.1 %collective-permute-start.1 = (f32[32,1,16,128]{3,0,1,2:T(8,128)}, f32[32,1,16,128]{3,0,1,2:T(8,128)}, u32[]{:S(2)}, u32[]{:S(2)}) collective-permute-start(f32[32,1,16,128]{3,0,1,2:T(8,128)} %get-tuple-element.495), channel_id=1, source_target_pairs={{0,16},{16,32},{32,48},{48,64},{64,80},{80,96},{96,112},{112,128},... | collective-permute-start | bytes 786440 | tf_op jit(solution)/shard_map/ppermute | solution.py:61
  18.5 29.0 %all-gather = f32[16,1,3072]{2,1,0:T(1,128)S(1)} all-gather(f32[1,1,3072]{2,1,0:T(1,128)S(1)} %maximum_bitcast_fusion), channel_id=1, replica_groups=mesh['space'=32,'field'=16] {'field'}, dimensions={0}, use_global_device_ids=true | all-gather | bytes 208896 | tf_op jit(solution)/shard_map/all_gather | solution.py:15
  47.7 1.6 fusion.91
  49.4 1.1 broadcast_in_dim.16
  50.5 6.5 %all-to-all-start.1 = ((f32[16,32,4,1,128]{4,1,2,3,0:T(8,128)}), f32[16,32,4,1,128]{4,1,2,3,0:T(8,128)S(1)}, u32[]{:S(2)}, u32[]{:S(2)}) async-start(f32[16,32,4,1,128]{4,1,2,3,0:T(8,128)} %broadcast_in_dim.16), calls=%async_computation.1 | async-start | bytes 2097152 | tf_op jit(solution)/shard_map/all_to_all | solution.py:45
  57.0 1.4 fusion.93
  58.4 1.7 fusion.94
  62.6 9.4 %all-to-all-done.1 = f32[16,32,4,1,128]{4,1,2,3,0:T(8,128)S(1)} async-done(((f32[16,32,4,1,128]{4,1,2,3,0:T(8,128)}), f32[16,32,4,1,128]{4,1,2,3,0:T(8,128)S(1)}, u32[]{:S(2)}, u32[]{:S(2)}) %all-to-all-start.1) | async-done | bytes 1048608 | tf_op jit(solution)/shard_map/all_to_all | solution.py:45
  72.1 4.1 %fusion.81 = f32[32,4,16,128]{3,0,1,2:T(8,128)} fusion(f32[32,4,16,128]{3,0,1,2:T(8,128)S(1)} %bitcast.411, f32[16,32,4,1,128]{4,1,2,3,0:T(8,128)S(1)} %all-to-all-done.1, f32[32,4,16,127]{3,0,1,2:T(8,128)} %get-tuple-element.502, f32[32,4,16,1]{3,0,1,2:T(8,128)} %get-tuple-element.504, f32[32,4,16,1]{3,0,1,2:T(8,128)} %get-tuple-element.503, ...), kind=kLoop, calls=%fused_computation.127 | loop fusion | flops 8912896 | bytes 8060940 | tf_op jit(solution)/shard_map/sub | solution.py:82
  76.2 36.8 %while.30 = (s32[]{:T(128)}, f32[32,4,16,128]{3,0,1,2:T(8,128)}, f32[206]{0:T(256)S(1)}, f32[206,1]{0,1:T(1,128)S(1)}, f32[4,16,128]{2,1,0:T(8,128)S(1)}, /*inde...) while((s32[]{:T(128)}, f32[32,4,16,128]{3,0,1,2:T(8,128)}, ...), condition=%wide.region_2.3_spmd, body=%wide.region_1.2_spmd.sunk | while | flops 427352064 | bytes 23221052 | solution.py:126
  77.8 1.0 fusion.206
  96.2 1.0 fusion.206
  105.4 1.0 fusion.206
  113.0 6.6 %all-to-all-start.2 = ((f32[16,32,4,1,128]{4,1,2,3,0:T(8,128)}), f32[16,32,4,1,128]{4,1,2,3,0:T(8,128)S(1)}, u32[]{:S(2)}, u32[]{:S(2)}) async-start(f32[16,32,4,1,128]{4,1,2,3,0:T(8,128)} %bitcast.59), calls=%async_computation.2 | async-start | bytes 2097152 | tf_op jit(solution)/shard_map/all_to_all | solution.py:33
  121.5 1.9 fusion.88
  123.4 11.2 %all-to-all-done.2 = f32[16,32,4,1,128]{4,1,2,3,0:T(8,128)S(1)} async-done(((f32[16,32,4,1,128]{4,1,2,3,0:T(8,128)}), f32[16,32,4,1,128]{4,1,2,3,0:T(8,128)S(1)}, u32[]{:S(2)}, u32[]{:S(2)}) %all-to-all-start.2) | async-done | bytes 1048608 | tf_op jit(solution)/shard_map/all_to_all | solution.py:33
  134.7 1.1 broadcast_in_dim.17
  135.8 6.6 %all-to-all-start.3 = ((f32[16,32,4,1,128]{4,1,2,3,0:T(8,128)}), f32[16,32,4,1,128]{4,1,2,3,0:T(8,128)S(1)}, u32[]{:S(2)}, u32[]{:S(2)}) async-start(f32[16,32,4,1,128]{4,1,2,3,0:T(8,128)} %broadcast_in_dim.17), calls=%async_computation.3 | async-start | bytes 2097152 | tf_op jit(solution)/shard_map/all_to_all | solution.py:45
  142.4 1.1 fusion.85
  143.5 6.5 %collective-permute-start.2 = (f32[32,1,16,128]{3,0,1,2:T(8,128)S(1)}, f32[32,1,16,128]{3,0,1,2:T(8,128)S(1)}, u32[]{:S(2)}, u32[]{:S(2)}) collective-permute-start(f32[32,1,16,128]{3,0,1,2:T(8,128)S(1)} %get-tuple-element.486), channel_id=1, source_target_pairs={{16,0},{32,16},{48,32},{64,48},{80,64},{96,80},{112,96},{128,112},... | collective-permute-start | bytes 786440 | tf_op jit(solution)/shard_map/ppermute | solution.py:62
  150.1 2.1 %collective-permute-start.3 = (f32[32,1,16,128]{3,0,1,2:T(8,128)S(1)}, f32[32,1,16,128]{3,0,1,2:T(8,128)}, u32[]{:S(2)}, u32[]{:S(2)}) collective-permute-start(f32[32,1,16,128]{3,0,1,2:T(8,128)S(1)} %get-tuple-element.485), channel_id=1, source_target_pairs={{0,16},{16,32},{32,48},{48,64},{64,80},{80,96},{96,112},{112,128},... | collective-permute-start | bytes 786440 | tf_op jit(solution)/shard_map/ppermute | solution.py:61
  152.2 3.3 %fusion.89 = (f32[32,4,16,1]{3,0,1,2:T(8,128)}, f32[32,4,16,1]{3,0,1,2:T(8,128)}) fusion(f32[32,4,16,128]{3,0,1,2:T(8,128)} %get-tuple-element.387), kind=kLoop, calls=%fused_computation.145 | loop fusion | bytes 32768 | tf_op jit(solution)/shard_map/jit(_roll_static)/slice | solution.py:72
  155.4 3.1 %fusion.86 = (f32[32,4,15,128]{3,0,1,2:T(8,128)}, f32[32,4,15,128]{3,0,1,2:T(8,128)}) fusion(f32[32,4,16,128]{3,0,1,2:T(8,128)} %get-tuple-element.387), kind=kLoop, calls=%fused_computation.142 | loop fusion | bytes 3932160 | tf_op jit(solution)/shard_map/jit(_roll_static)/slice | solution.py:70
  160.7 10.1 %collective-permute-done.3 = f32[32,1,16,128]{3,0,1,2:T(8,128)} collective-permute-done((f32[32,1,16,128]{3,0,1,2:T(8,128)S(1)}, f32[32,1,16,128]{3,0,1,2:T(8,128)}, u32[]{:S(2)}, u32[]{:S(2)}) %collective-permute-start.3) | collective-permute-done | bytes 262176 | tf_op jit(solution)/shard_map/ppermute | solution.py:61
  170.8 3.8 %fusion.79 = f32[32,4,16,128]{3,0,1,2:T(8,128)S(1)} fusion(f32[32,4,16,128]{3,0,1,2:T(8,128)} %get-tuple-element.387, f32[16,32,4,1,128]{4,1,2,3,0:T(8,128)S(1)} %all-to-all-done.3, f32[32,4,16,127]{3,0,1,2:T(8,128)S(1)} %get-tuple-element.492, f32[32,4,16,1]{3,0,1,2:T(8,128)} %get-tuple-element.494, f32[32,4,16,1]{3,0,1,2:T(8,128)} %get-tuple-element.493, ...), kind=kLoop, calls=%fused_computation.124 | loop fusion | flops 8912896 | bytes 8060940 | tf_op jit(solution)/shard_map/sub | solution.py:82
  175.3 29.3 %while.31 = (s32[]{:T(128)}, f32[32,4,16,128]{3,2,1,0:T(8,128)S(1)}, f32[206]{0:T(256)S(1)}, f32[206,1]{0,1:T(1,128)S(1)}, f32[4,16,128]{2,1,0:T(8,128)S(1)}, /*...) while((s32[]{:T(128)}, ...), condition=%wide.region_5.6_spmd, body=%wide.region_4.5_spmd.sunk | while | flops 427352064 | bytes 22644000 | solution.py:126
  183.1 1.0 fusion.234
  190.4 1.0 fusion.234
  197.8 1.0 fusion.234
  (171 shorter events, 65.6 us)
Async XLA Ops:
  0.0 10.1 %copy-start.2 = (f32[1,32,4,16,128]{4,3,2,1,0:T(8,128)S(1)}, f32[1,32,4,16,128]{4,3,2,1,0:T(8,128)}, u32[]{:S(2)}) copy-start(f32[1,32,4,16,128]{4,3,2,1,0:T(8,128)} %param.15) | copy-start | bytes 3145732
  2.7 46.6 %all-to-all-start = ((f32[16,32,4,1,128]{4,2,1,3,0:T(4,128)}), f32[16,32,4,1,128]{4,2,1,3,0:T(4,128)S(1)}, u32[]{:S(2)}, u32[]{:S(2)}) async-start(f32[16,32,4,1,128]{4,2,1,3,0:T(4,128)} %bitcast.249), calls=%async_computation | async-start | bytes 2097152 | tf_op jit(solution)/shard_map/all_to_all | solution.py:33
  10.1 8.3 %copy-start.5 = (f32[3,4,1,128]{3,2,1,0:T(1,128)S(1)}, f32[3,4,1,128]{3,2,1,0:T(1,128)}, u32[]{:S(2)}) copy-start(f32[3,4,1,128]{3,2,1,0:T(1,128)} %param.16) | copy-start | bytes 18436
  10.2 8.3 %copy-start.6 = (f32[4,1,128]{2,1,0:T(1,128)S(1)}, f32[4,1,128]{2,1,0:T(1,128)}, u32[]{:S(2)}) copy-start(f32[4,1,128]{2,1,0:T(1,128)} %param.19) | copy-start | bytes 6148
  10.2 8.3 %copy-start.7 = (f32[4,1,128]{2,1,0:T(1,128)S(1)}, f32[4,1,128]{2,1,0:T(1,128)}, u32[]{:S(2)}) copy-start(f32[4,1,128]{2,1,0:T(1,128)} %param.18) | copy-start | bytes 6148
  10.2 8.3 %copy-start.8 = (f32[4,1,128]{2,1,0:T(1,128)S(1)}, f32[4,1,128]{2,1,0:T(1,128)}, u32[]{:S(2)}) copy-start(f32[4,1,128]{2,1,0:T(1,128)} %param.17) | copy-start | bytes 6148
  11.7 50.9 %collective-permute-start = (f32[32,1,16,128]{3,0,1,2:T(8,128)}, f32[32,1,16,128]{3,0,1,2:T(8,128)}, u32[]{:S(2)}, u32[]{:S(2)}) collective-permute-start(f32[32,1,16,128]{3,0,1,2:T(8,128)} %get-tuple-element.496), channel_id=1, source_target_pairs={{16,0},{32,16},{48,32},{64,48},{80,64},{96,80},{112,96},{128,112},... | collective-permute-start | bytes 786440 | tf_op jit(solution)/shard_map/ppermute | solution.py:62
  16.3 46.3 %collective-permute-start.1 = (f32[32,1,16,128]{3,0,1,2:T(8,128)}, f32[32,1,16,128]{3,0,1,2:T(8,128)}, u32[]{:S(2)}, u32[]{:S(2)}) collective-permute-start(f32[32,1,16,128]{3,0,1,2:T(8,128)} %get-tuple-element.495), channel_id=1, source_target_pairs={{0,16},{16,32},{32,48},{48,64},{64,80},{80,96},{96,112},{112,128},... | collective-permute-start | bytes 786440 | tf_op jit(solution)/shard_map/ppermute | solution.py:61
  50.5 21.5 %all-to-all-start.1 = ((f32[16,32,4,1,128]{4,1,2,3,0:T(8,128)}), f32[16,32,4,1,128]{4,1,2,3,0:T(8,128)S(1)}, u32[]{:S(2)}, u32[]{:S(2)}) async-start(f32[16,32,4,1,128]{4,1,2,3,0:T(8,128)} %broadcast_in_dim.16), calls=%async_computation.1 | async-start | bytes 2097152 | tf_op jit(solution)/shard_map/all_to_all | solution.py:45
  58.4 1.7 copy-start.4
  58.4 4.2 %copy-start.9 = (f32[206]{0:T(256)S(1)}, f32[206]{0:T(256)}, u32[]{:S(2)}) copy-start(f32[206]{0:T(256)} %param.25) | copy-start | bytes 2476
  72.1 4.1 %copy-start = (bf16[206,32]{0,1:T(8,128)(2,1)S(1)}, bf16[206,32]{0,1:T(8,128)(2,1)}, u32[]{:S(2)}) copy-start(bf16[206,32]{0,1:T(8,128)(2,1)} %param.21) | copy-start | bytes 39556
  72.1 4.1 %copy-start.10 = (bf16[206,32]{0,1:T(8,128)(2,1)S(1)}, bf16[206,32]{0,1:T(8,128)(2,1)}, u32[]{:S(2)}) copy-start(bf16[206,32]{0,1:T(8,128)(2,1)} %param.22) | copy-start | bytes 39556
  72.1 4.1 %copy-start.13 = (f32[206]{0:T(256)S(1)}, f32[206]{0:T(256)}, u32[]{:S(2)}) copy-start(f32[206]{0:T(256)} %param.24) | copy-start | bytes 2476
  76.2 1.6 copy-start.11
  85.4 1.6 copy-start.11
  94.6 1.6 copy-start.11
  103.8 1.6 copy-start.11
  113.0 21.7 %all-to-all-start.2 = ((f32[16,32,4,1,128]{4,1,2,3,0:T(8,128)}), f32[16,32,4,1,128]{4,1,2,3,0:T(8,128)S(1)}, u32[]{:S(2)}, u32[]{:S(2)}) async-start(f32[16,32,4,1,128]{4,1,2,3,0:T(8,128)} %bitcast.59), calls=%async_computation.2 | async-start | bytes 2097152 | tf_op jit(solution)/shard_map/all_to_all | solution.py:33
  135.8 35.0 %all-to-all-start.3 = ((f32[16,32,4,1,128]{4,1,2,3,0:T(8,128)}), f32[16,32,4,1,128]{4,1,2,3,0:T(8,128)S(1)}, u32[]{:S(2)}, u32[]{:S(2)}) async-start(f32[16,32,4,1,128]{4,1,2,3,0:T(8,128)} %broadcast_in_dim.17), calls=%async_computation.3 | async-start | bytes 2097152 | tf_op jit(solution)/shard_map/all_to_all | solution.py:45
  143.5 16.5 %collective-permute-start.2 = (f32[32,1,16,128]{3,0,1,2:T(8,128)S(1)}, f32[32,1,16,128]{3,0,1,2:T(8,128)S(1)}, u32[]{:S(2)}, u32[]{:S(2)}) collective-permute-start(f32[32,1,16,128]{3,0,1,2:T(8,128)S(1)} %get-tuple-element.486), channel_id=1, source_target_pairs={{16,0},{32,16},{48,32},{64,48},{80,64},{96,80},{112,96},{128,112},... | collective-permute-start | bytes 786440 | tf_op jit(solution)/shard_map/ppermute | solution.py:62
  150.1 20.8 %collective-permute-start.3 = (f32[32,1,16,128]{3,0,1,2:T(8,128)S(1)}, f32[32,1,16,128]{3,0,1,2:T(8,128)}, u32[]{:S(2)}, u32[]{:S(2)}) collective-permute-start(f32[32,1,16,128]{3,0,1,2:T(8,128)S(1)} %get-tuple-element.485), channel_id=1, source_target_pairs={{0,16},{16,32},{32,48},{48,64},{64,80},{80,96},{96,112},{112,128},... | collective-permute-start | bytes 786440 | tf_op jit(solution)/shard_map/ppermute | solution.py:61
  160.0 0.7 copy-start.3
  174.6 0.7 copy-start.12
  204.6 1.0 copy-start.1
where the time goes:
time: 206 us
  matrix products  56.8 us (28%)
  starting transfers between devices  42.5 us (21%)
  local copies, waits for them, and re-layouts  32.8 us (16%)
  waiting for transfers between devices  31.4 us (15%)
  blocking collectives  29 us (14%)
  other arithmetic  8.22 us (4%)
  between operations  4.04 us (2%)
    dot_general x40, matrix products, react(): jnp.dot(species_yield_weights, rates, preferred_element_type=jnp.float32)  40.1 us
    all_gather x1, blocking collectives, turned_gather(): result = lax.all_gather(both, axis, axis=0, tiled=True)  29 us
    dot_general x40, matrix products, react(): jnp.dot(left_bilinear_weights, lowered, preferred_element_type=jnp.float32)  16.6 us
    all_to_all x2, starting transfers between devices, sent_and_summed(): lax.all_to_all(tiles, axis, split_axis=0, concat_axis=0, tiled=True)  14 us
    all_to_all x2, starting transfers between devices, from_everyone(): lax.all_to_all(jnp.broadcast_to(value[None], (count, *value.shape)), axis...  13.1 us
    all_to_all x2, waiting for transfers between devices, sent_and_summed(): lax.all_to_all(tiles, axis, split_axis=0, concat_axis=0, tiled=True)  11.2 us
    ppermute x2, starting transfers between devices, extended(): after = lax.ppermute(leading, axis, down)  11.1 us
    ppermute x2, waiting for transfers between devices, extended(): before = lax.ppermute(last, axis, up)  10.1 us
  transfers between devices with their start and end apart: 8, of which 4 were waited for; matrix products, arithmetic and copies ran while one was open for 9% of the time, Pallas kernels for 0%

commit v1 on v0

--- a/solution.py
+++ b/solution.py
@@ -12,7 +12,9 @@
     turned = [jnp.moveaxis(a, dim, 0) for a, dim in zip(arrays, dims)]
     widths = [t[0].size for t in turned]
     both = jnp.concatenate([t.reshape(-1, w) for t, w in zip(turned, widths)], axis=1)
-    result = lax.all_gather(both, axis, axis=0, tiled=True)
+    result = jnp.concatenate(
+        lax.all_to_all(jnp.stack([both] * lax.axis_size(axis)), axis, 0, 0), axis=0
+    )
     tiles = jnp.split(result, [sum(widths[:k]) for k in range(1, len(widths))], axis=1)
     return tuple(
         (

time: 206 us -> 227 us (1.10)
  blocking collectives: 29 us -> 0 us
  matrix products: 56.8 us -> 83.3 us
  starting transfers between devices: 42.5 us -> 52.1 us
  waiting for transfers between devices: 31.4 us -> 40.5 us
  local copies, waits for them, and re-layouts: 32.8 us -> 35.7 us
    all_gather x1 -> x0, blocking collectives: 29 us -> none  [turned_gather(): result = lax.all_gather(both, axis, axis=0, tiled=True)]
    dot_general x40, matrix products: 40.1 us -> 66.7 us  [react(): jnp.dot(species_yield_weights, rates, preferred_element_type=jnp.float32)]
    all_to_all x0 -> x1, starting transfers between devices: none -> 6.6 us  [turned_gather(): lax.all_to_all(jnp.stack([both] * lax.axis_size(axis)), axis, 0, 0)]
    all_to_all x0 -> x1, waiting for transfers between devices: none -> 6.18 us  [turned_gather(): lax.all_to_all(jnp.stack([both] * lax.axis_size(axis)), axis, 0, 0)]
    ppermute x2, starting transfers between devices: 11.1 us -> 14.2 us  [extended(): after = lax.ppermute(leading, axis, down)]
    unnamed x29 -> x35, local copies, waits for them, and re-layouts: 5.16 us -> 5.15 us
  transfers between devices with their start and end apart: 8 -> 9, of which waited for: 4 -> 5; matrix products, arithmetic and copies ran while one was open for 9% -> 10% of each run, Pallas kernels for 0% -> 0%
where the time goes in v1:
time: 227 us; the launch traced here: 225 us
  matrix products  83.3 us (37%)
  starting transfers between devices  52.1 us (23%)
  waiting for transfers between devices  40.5 us (18%)
  local copies, waits for them, and re-layouts  35.7 us (16%)
  other arithmetic  8.87 us (4%)
  between operations  3.99 us (2%)
    dot_general x40, matrix products, react(): jnp.dot(species_yield_weights, rates, preferred_element_type=jnp.float32)  66.7 us
    dot_general x40, matrix products, react(): jnp.dot(left_bilinear_weights, lowered, preferred_element_type=jnp.float32)  16.6 us
    ppermute x2, starting transfers between devices, extended(): after = lax.ppermute(leading, axis, down)  14.2 us
    all_to_all x2, starting transfers between devices, sent_and_summed(): lax.all_to_all(tiles, axis, split_axis=0, concat_axis=0, tiled=True)  14.1 us
    all_to_all x2, starting transfers between devices, from_everyone(): lax.all_to_all(jnp.broadcast_to(value[None], (count, *value.shape)), axis...  13.1 us
    all_to_all x2, waiting for transfers between devices, sent_and_summed(): lax.all_to_all(tiles, axis, split_axis=0, concat_axis=0, tiled=True)  12 us
    all_to_all x2, waiting for transfers between devices, from_everyone(): lax.all_to_all(jnp.broadcast_to(value[None], (count, *value.shape)), axis...  11.6 us
    ppermute x2, waiting for transfers between devices, extended(): before = lax.ppermute(last, axis, up)  10.7 us
  transfers between devices with their start and end apart: 9, of which 5 were waited for; matrix products, arithmetic and copies ran while one was open for 10% of the time, Pallas kernels for 0%

profile of v1, /device:TPU:6, one launch (start us, length us, event | category | flops | bytes accessed | tf_op | source)
XLA Modules:
  0.0 225.3 jit_solution(11896537235234123455)
XLA Ops:
  0.0 2.7 %copy.133 = f32[1,32,4,16,128]{4,2,1,3,0:T(4,128)} copy(f32[1,32,4,16,128]{4,3,2,1,0:T(8,128)} %param.15) | data formatting | bytes 2097152 | tf_op args[0]
  2.7 7.5 %all-to-all-start.1 = ((f32[16,32,4,1,128]{4,2,1,3,0:T(4,128)}), f32[16,32,4,1,128]{4,2,1,3,0:T(4,128)S(1)}, u32[]{:S(2)}, u32[]{:S(2)}) async-start(f32[16,32,4,1,128]{4,2,1,3,0:T(4,128)} %bitcast.248), calls=%async_computation.1 | async-start | bytes 2097152 | tf_op jit(solution)/shard_map/all_to_all | solution.py:35
  11.6 4.6 %collective-permute-start = (f32[32,1,16,128]{3,0,1,2:T(8,128)}, f32[32,1,16,128]{3,0,1,2:T(8,128)}, u32[]{:S(2)}, u32[]{:S(2)}) collective-permute-start(f32[32,1,16,128]{3,0,1,2:T(8,128)} %get-tuple-element.496), channel_id=1, source_target_pairs={{16,0},{32,16},{48,32},{64,48},{80,64},{96,80},{112,96},{128,112},... | collective-permute-start | bytes 786440 | tf_op jit(solution)/shard_map/ppermute | solution.py:64
  16.3 2.1 collective-permute-start.1
  26.6 6.6 %all-to-all-start = ((f32[16,1,3072]{2,1,0:T(1,128)}), f32[16,1,3072]{2,1,0:T(1,128)S(1)}, u32[]{:S(2)}, u32[]{:S(2)}) async-start(f32[16,1,3072]{2,1,0:T(1,128)} %stack.2), calls=%async_computation | async-start | bytes 393216 | tf_op jit(solution)/shard_map/all_to_all | solution.py:16
  33.3 6.2 %all-to-all-done = f32[16,1,3072]{2,1,0:T(1,128)S(1)} async-done(((f32[16,1,3072]{2,1,0:T(1,128)}), f32[16,1,3072]{2,1,0:T(1,128)S(1)}, u32[]{:S(2)}, u32[]{:S(2)}) %all-to-all-start) | async-done | bytes 196640 | tf_op jit(solution)/shard_map/all_to_all | solution.py:16
  40.6 6.5 %all-to-all-start.2 = ((f32[16,32,4,1,128]{4,1,2,3,0:T(8,128)}), f32[16,32,4,1,128]{4,1,2,3,0:T(8,128)S(1)}, u32[]{:S(2)}, u32[]{:S(2)}) async-start(f32[16,32,4,1,128]{4,1,2,3,0:T(8,128)} %broadcast_in_dim.16), calls=%async_computation.2 | async-start | bytes 2097152 | tf_op jit(solution)/shard_map/all_to_all | solution.py:47
  47.1 1.7 fusion.94
  50.5 11.6 %all-to-all-done.2 = f32[16,32,4,1,128]{4,1,2,3,0:T(8,128)S(1)} async-done(((f32[16,32,4,1,128]{4,1,2,3,0:T(8,128)}), f32[16,32,4,1,128]{4,1,2,3,0:T(8,128)S(1)}, u32[]{:S(2)}, u32[]{:S(2)}) %all-to-all-start.2) | async-done | bytes 1048608 | tf_op jit(solution)/shard_map/all_to_all | solution.py:47
  62.2 4.2 %fusion.81 = f32[32,4,16,128]{3,0,1,2:T(8,128)} fusion(f32[32,4,16,128]{3,0,1,2:T(8,128)S(1)} %bitcast.410, f32[16,32,4,1,128]{4,1,2,3,0:T(8,128)S(1)} %all-to-all-done.2, f32[32,4,16,127]{3,0,1,2:T(8,128)} %get-tuple-element.502, f32[32,4,16,1]{3,0,1,2:T(8,128)} %get-tuple-element.504, f32[32,4,16,1]{3,0,1,2:T(8,128)} %get-tuple-element.503, ...), kind=kLoop, calls=%fused_computation.127 | loop fusion | flops 8912896 | bytes 8060940 | tf_op jit(solution)/shard_map/sub | solution.py:84
  66.4 49.9 %while.30 = (s32[]{:T(128)}, f32[32,4,16,128]{3,0,1,2:T(8,128)}, f32[206]{0:T(256)S(1)}, f32[206,1]{0,1:T(1,128)}, f32[4,16,128]{2,1,0:T(8,128)S(1)}, /*index=5*...) while((s32[]{:T(128)}, f32[32,4,16,128]{3,0,1,2:T(8,128)}, ...), condition=%wide.region_2.3_spmd, body=%wide.region_1.2_spmd.sunk | while | flops 427352064 | bytes 23168288 | solution.py:128
  68.0 1.7 fusion.206
  76.4 1.7 fusion.210
  80.5 1.7 fusion.206
  82.6 1.7 fusion.207
  93.0 1.7 fusion.206
  105.4 1.7 fusion.206
  116.3 6.6 %all-to-all-start.3 = ((f32[16,32,4,1,128]{4,1,2,3,0:T(8,128)}), f32[16,32,4,1,128]{4,1,2,3,0:T(8,128)S(1)}, u32[]{:S(2)}, u32[]{:S(2)}) async-start(f32[16,32,4,1,128]{4,1,2,3,0:T(8,128)} %bitcast.59), calls=%async_computation.3 | async-start | bytes 2097152 | tf_op jit(solution)/shard_map/all_to_all | solution.py:35
  124.8 1.9 fusion.88
  126.7 11.3 %all-to-all-done.3 = f32[16,32,4,1,128]{4,1,2,3,0:T(8,128)S(1)} async-done(((f32[16,32,4,1,128]{4,1,2,3,0:T(8,128)}), f32[16,32,4,1,128]{4,1,2,3,0:T(8,128)S(1)}, u32[]{:S(2)}, u32[]{:S(2)}) %all-to-all-start.3) | async-done | bytes 1048608 | tf_op jit(solution)/shard_map/all_to_all | solution.py:35
  139.2 6.6 %all-to-all-start.4 = ((f32[16,32,4,1,128]{4,1,2,3,0:T(8,128)}), f32[16,32,4,1,128]{4,1,2,3,0:T(8,128)S(1)}, u32[]{:S(2)}, u32[]{:S(2)}) async-start(f32[16,32,4,1,128]{4,1,2,3,0:T(8,128)} %broadcast_in_dim.17), calls=%async_computation.4 | async-start | bytes 2097152 | tf_op jit(solution)/shard_map/all_to_all | solution.py:47
  146.9 9.6 %collective-permute-start.2 = (f32[32,1,16,128]{3,0,1,2:T(8,128)S(1)}, f32[32,1,16,128]{3,0,1,2:T(8,128)S(1)}, u32[]{:S(2)}, u32[]{:S(2)}) collective-permute-start(f32[32,1,16,128]{3,0,1,2:T(8,128)S(1)} %get-tuple-element.486), channel_id=1, source_target_pairs={{16,0},{32,16},{48,32},{64,48},{80,64},{96,80},{112,96},{128,112},... | collective-permute-start | bytes 786440 | tf_op jit(solution)/shard_map/ppermute | solution.py:64
  156.5 2.1 collective-permute-start.3
  158.6 3.3 %fusion.89 = (f32[32,4,16,1]{3,0,1,2:T(8,128)}, f32[32,4,16,1]{3,0,1,2:T(8,128)}) fusion(f32[32,4,16,128]{3,0,1,2:T(8,128)} %get-tuple-element.387), kind=kLoop, calls=%fused_computation.145 | loop fusion | bytes 32768 | tf_op jit(solution)/shard_map/jit(_roll_static)/slice | solution.py:74
  161.8 3.1 %fusion.86 = (f32[32,4,15,128]{3,0,1,2:T(8,128)}, f32[32,4,15,128]{3,0,1,2:T(8,128)}) fusion(f32[32,4,16,128]{3,0,1,2:T(8,128)} %get-tuple-element.387), kind=kLoop, calls=%fused_computation.142 | loop fusion | bytes 3932160 | tf_op jit(solution)/shard_map/jit(_roll_static)/slice | solution.py:72
  166.5 10.7 %collective-permute-done.3 = f32[32,1,16,128]{3,0,1,2:T(8,128)} collective-permute-done((f32[32,1,16,128]{3,0,1,2:T(8,128)S(1)}, f32[32,1,16,128]{3,0,1,2:T(8,128)}, u32[]{:S(2)}, u32[]{:S(2)}) %collective-permute-start.3) | collective-permute-done | bytes 262176 | tf_op jit(solution)/shard_map/ppermute | solution.py:63
  177.2 3.8 %fusion.79 = f32[32,4,16,128]{3,0,1,2:T(8,128)S(1)} fusion(f32[32,4,16,128]{3,0,1,2:T(8,128)} %get-tuple-element.387, f32[16,32,4,1,128]{4,1,2,3,0:T(8,128)S(1)} %all-to-all-done.4, f32[32,4,16,127]{3,0,1,2:T(8,128)S(1)} %get-tuple-element.492, f32[32,4,16,1]{3,0,1,2:T(8,128)} %get-tuple-element.494, f32[32,4,16,1]{3,0,1,2:T(8,128)} %get-tuple-element.493, ...), kind=kLoop, calls=%fused_computation.124 | loop fusion | flops 8912896 | bytes 8060940 | tf_op jit(solution)/shard_map/sub | solution.py:84
  181.8 42.5 %while.31 = (s32[]{:T(128)}, f32[32,4,16,128]{3,2,1,0:T(8,128)S(1)}, f32[206]{0:T(256)S(1)}, f32[206,1]{0,1:T(1,128)}, f32[4,16,128]{2,1,0:T(8,128)S(1)}, /*inde...) while((s32[]{:T(128)}, ...), condition=%wide.region_5.6_spmd, body=%wide.region_4.5_spmd.sunk | while | flops 427352064 | bytes 22644000 | solution.py:128
  182.2 1.7 fusion.234
  192.9 1.7 fusion.234
  203.5 1.7 fusion.234
  214.1 1.7 fusion.234
  (171 shorter events, 91.2 us)
Async XLA Ops:
  0.0 10.1 %copy-start.2 = (f32[1,32,4,16,128]{4,3,2,1,0:T(8,128)S(1)}, f32[1,32,4,16,128]{4,3,2,1,0:T(8,128)}, u32[]{:S(2)}) copy-start(f32[1,32,4,16,128]{4,3,2,1,0:T(8,128)} %param.15) | copy-start | bytes 3145732
  2.7 23.1 %all-to-all-start.1 = ((f32[16,32,4,1,128]{4,2,1,3,0:T(4,128)}), f32[16,32,4,1,128]{4,2,1,3,0:T(4,128)S(1)}, u32[]{:S(2)}, u32[]{:S(2)}) async-start(f32[16,32,4,1,128]{4,2,1,3,0:T(4,128)} %bitcast.248), calls=%async_computation.1 | async-start | bytes 2097152 | tf_op jit(solution)/shard_map/all_to_all | solution.py:35
  10.1 8.9 %copy-start.4 = (f32[2,1,3]{2,1,0:T(1,128)S(1)}, f32[2,1,3]{2,1,0:T(1,128)}, u32[]{:S(2)}) copy-start(f32[2,1,3]{2,1,0:T(1,128)} %param.20) | copy-start | bytes 76
  10.2 11.5 %copy-start.9 = (f32[206]{0:T(256)S(1)}, f32[206]{0:T(256)}, u32[]{:S(2)}) copy-start(f32[206]{0:T(256)} %param.25) | copy-start | bytes 2476
  11.6 38.9 %collective-permute-start = (f32[32,1,16,128]{3,0,1,2:T(8,128)}, f32[32,1,16,128]{3,0,1,2:T(8,128)}, u32[]{:S(2)}, u32[]{:S(2)}) collective-permute-start(f32[32,1,16,128]{3,0,1,2:T(8,128)} %get-tuple-element.496), channel_id=1, source_target_pairs={{16,0},{32,16},{48,32},{64,48},{80,64},{96,80},{112,96},{128,112},... | collective-permute-start | bytes 786440 | tf_op jit(solution)/shard_map/ppermute | solution.py:64
  16.3 34.3 %collective-permute-start.1 = (f32[32,1,16,128]{3,0,1,2:T(8,128)}, f32[32,1,16,128]{3,0,1,2:T(8,128)}, u32[]{:S(2)}, u32[]{:S(2)}) collective-permute-start(f32[32,1,16,128]{3,0,1,2:T(8,128)} %get-tuple-element.495), channel_id=1, source_target_pairs={{0,16},{16,32},{32,48},{48,64},{64,80},{80,96},{96,112},{112,128},... | collective-permute-start | bytes 786440 | tf_op jit(solution)/shard_map/ppermute | solution.py:63
  23.8 1.4 copy-start.5
  23.8 1.4 copy-start.6
  23.8 1.4 copy-start.7
  23.8 1.4 copy-start.8
  26.6 13.0 %all-to-all-start = ((f32[16,1,3072]{2,1,0:T(1,128)}), f32[16,1,3072]{2,1,0:T(1,128)S(1)}, u32[]{:S(2)}, u32[]{:S(2)}) async-start(f32[16,1,3072]{2,1,0:T(1,128)} %stack.2), calls=%async_computation | async-start | bytes 393216 | tf_op jit(solution)/shard_map/all_to_all | solution.py:16
  40.6 21.5 %all-to-all-start.2 = ((f32[16,32,4,1,128]{4,1,2,3,0:T(8,128)}), f32[16,32,4,1,128]{4,1,2,3,0:T(8,128)S(1)}, u32[]{:S(2)}, u32[]{:S(2)}) async-start(f32[16,32,4,1,128]{4,1,2,3,0:T(8,128)} %broadcast_in_dim.16), calls=%async_computation.2 | async-start | bytes 2097152 | tf_op jit(solution)/shard_map/all_to_all | solution.py:47
  62.1 4.2 %copy-start = (bf16[206,32]{0,1:T(8,128)(2,1)S(1)}, bf16[206,32]{0,1:T(8,128)(2,1)}, u32[]{:S(2)}) copy-start(bf16[206,32]{0,1:T(8,128)(2,1)} %param.21) | copy-start | bytes 39556
  62.1 4.2 %copy-start.10 = (bf16[206,32]{0,1:T(8,128)(2,1)S(1)}, bf16[206,32]{0,1:T(8,128)(2,1)}, u32[]{:S(2)}) copy-start(bf16[206,32]{0,1:T(8,128)(2,1)} %param.22) | copy-start | bytes 39556
  62.2 4.2 %copy-start.12 = (bf16[32,206]{1,0:T(8,128)(2,1)S(1)}, bf16[32,206]{1,0:T(8,128)(2,1)}, u32[]{:S(2)}) copy-start(bf16[32,206]{1,0:T(8,128)(2,1)} %param.23) | copy-start | bytes 39556
  62.2 4.2 %copy-start.14 = (f32[206]{0:T(256)S(1)}, f32[206]{0:T(256)}, u32[]{:S(2)}) copy-start(f32[206]{0:T(256)} %param.24) | copy-start | bytes 2476
  116.3 21.7 %all-to-all-start.3 = ((f32[16,32,4,1,128]{4,1,2,3,0:T(8,128)}), f32[16,32,4,1,128]{4,1,2,3,0:T(8,128)S(1)}, u32[]{:S(2)}, u32[]{:S(2)}) async-start(f32[16,32,4,1,128]{4,1,2,3,0:T(8,128)} %bitcast.59), calls=%async_computation.3 | async-start | bytes 2097152 | tf_op jit(solution)/shard_map/all_to_all | solution.py:35
  139.2 38.0 %all-to-all-start.4 = ((f32[16,32,4,1,128]{4,1,2,3,0:T(8,128)}), f32[16,32,4,1,128]{4,1,2,3,0:T(8,128)S(1)}, u32[]{:S(2)}, u32[]{:S(2)}) async-start(f32[16,32,4,1,128]{4,1,2,3,0:T(8,128)} %broadcast_in_dim.17), calls=%async_computation.4 | async-start | bytes 2097152 | tf_op jit(solution)/shard_map/all_to_all | solution.py:47
  146.9 18.9 %collective-permute-start.2 = (f32[32,1,16,128]{3,0,1,2:T(8,128)S(1)}, f32[32,1,16,128]{3,0,1,2:T(8,128)S(1)}, u32[]{:S(2)}, u32[]{:S(2)}) collective-permute-start(f32[32,1,16,128]{3,0,1,2:T(8,128)S(1)} %get-tuple-element.486), channel_id=1, source_target_pairs={{16,0},{32,16},{48,32},{64,48},{80,64},{96,80},{112,96},{128,112},... | collective-permute-start | bytes 786440 | tf_op jit(solution)/shard_map/ppermute | solution.py:64
  156.5 20.8 %collective-permute-start.3 = (f32[32,1,16,128]{3,0,1,2:T(8,128)S(1)}, f32[32,1,16,128]{3,0,1,2:T(8,128)}, u32[]{:S(2)}, u32[]{:S(2)}) collective-permute-start(f32[32,1,16,128]{3,0,1,2:T(8,128)S(1)} %get-tuple-element.485), channel_id=1, source_target_pairs={{0,16},{16,32},{32,48},{48,64},{64,80},{80,96},{96,112},{112,128},... | collective-permute-start | bytes 786440 | tf_op jit(solution)/shard_map/ppermute | solution.py:63
  165.8 0.7 copy-start.3
  181.0 0.7 copy-start.11
  181.0 0.7 copy-start.13
  181.0 0.7 copy-start.15
  224.3 1.0 copy-start.1
